TPU v7x, 512 devices: a whole 4x8x8 slice. The times are simulated.
512 devices in a mesh: seq: 32 (over z_lo, y), blk: 8 (over x, core), grp: 2 (over z_hi).
Axes of the slice: x: 4, y: 8, z: 8 (z_hi: 2, z_lo: 4; z = z_hi * 4 + z_lo), core: 2. Of those that a mesh axis runs over, the one named last changes fastest.
Arguments:
- activations: bfloat16 [32768, 8192], P('seq', 'blk'), may hold values from -23 to 23
- cotangent: bfloat16 [32768, 1024], P('seq'), may hold values from -0.0625 to 0.0625
- factor: float32 [8192, 1024], P('blk', ('seq', 'grp')), may hold values from -0.3 to 1.7
Outputs:
- new_factor: float32 [8192, 1024], P('blk', ('seq', 'grp'))
- direction: float32 [8192, 1024], P('blk', ('seq', 'grp'))
All inputs are finite; a program needn't handle non-finite values.
Results may differ from a plain program's by a relative error of at most 0.007.
Values may be sent and summed in bfloat16 or wider, within the bound.
No kernel may reach another device: no remote copies, remote signals or barrier semaphores. Data moves between devices by JAX's collectives and lax.ppermute only.
A program may use at most 64 MiB of HBM per device.

v0:
```python
import functools

import jax
import jax.numpy as jnp
from jax import lax
from jax.experimental import pallas as pl
from jax.experimental.pallas import tpu as pltpu
from jax.sharding import Mesh
from jax.sharding import PartitionSpec as P


SEQ = ("seq_0", "seq_1")
SEQ_GRP = ("seq_0", "seq_1", "grp")
PLANES = ("seq_0", "seq_1", "blk", "grp")


damping = 0.25
step_size = 0.4

f32, bf16 = jnp.float32, jnp.bfloat16
VMEM_LIMIT = 16 * 1024 * 1024
ROWS_ROWS = (((1,), (1,)), ((), ()))
TOKENS_FIRST = (((0,), (0,)), ((), ()))

BLOCKS = 8


def device(z, y, blk):
    core = blk % 2
    z, y = (z - core) % 8, (y - core) % 8
    return ((z % 4 * 8 + y) * BLOCKS + blk) * 2 + z // 4


FAR_GROUPS = [
    [device(4 * h + 2 * zh + b, 2 * yh + a, blk) for yh in range(4) for zh in range(2)]
    for blk in range(BLOCKS)
    for h in range(2)
    for a in range(2)
    for b in range(2)
]


COSETS = [
    FAR_GROUPS[8 * blk + k] + FAR_GROUPS[8 * blk + 4 + k] for blk in range(BLOCKS) for k in range(4)
]


def moves(step_z, step_y):
    return [
        (device(z, y, blk), device(step_z(z), step_y(y), blk))
        for z in range(8)
        for y in range(8)
        for blk in range(BLOCKS)
    ]


def stay(at):
    return at


def inner(at):
    return at ^ 1


INNER = {1: moves(inner, stay), 2: moves(stay, inner), 3: moves(inner, inner)}
ORDER = (3, 2, 1)


def exchange(blocks, groups):
    return lax.all_to_all(
        blocks, PLANES, split_axis=0, concat_axis=0, tiled=True, axis_index_groups=groups
    )


def vmem():
    return pl.BlockSpec(memory_space=pltpu.VMEM)


def hbm():
    return pl.BlockSpec(memory_space=pltpu.HBM)


def run_copies(pairs, sems):
    copies = [pltpu.make_async_copy(*pair, sems.at[k]) for k, pair in enumerate(pairs)]
    for copy in copies:
        copy.start()
    return copies


def position():
    core = lax.axis_index("blk") & 1
    z = (lax.axis_index("grp") * 4 + lax.axis_index("seq_0") + core) & 7
    y = (lax.axis_index("seq_1") + core) & 7
    return core, y & 1, z & 1, y >> 1, (z & 3) >> 1, z >> 2


def call(kernel, out_shape, in_specs, out_specs, *args, **more):
    return pl.pallas_call(
        kernel,
        out_shape=out_shape,
        in_specs=in_specs,
        out_specs=out_specs,
        compiler_params=pltpu.CompilerParams(vmem_limit_bytes=VMEM_LIMIT),
        **more,
    )(*args)


def spread_kernel(far_own_ref, out_ref, own, low, sem, sems):
    arriving = pltpu.make_async_copy(far_own_ref, own, sem)
    arriving.start()
    arriving.wait()
    low[...] = own[...].astype(bf16)
    for copy in run_copies([(low, out_ref.at[k]) for k in range(out_ref.shape[0])], sems):
        copy.wait()


def spread(own, count):
    own = pltpu.with_memory_space_constraint(own, pltpu.HBM)
    shape = pltpu.HBM((count,) + own.shape, bf16)
    scratch = [
        pltpu.VMEM(own.shape, f32),
        pltpu.VMEM(own.shape, bf16),
        pltpu.SemaphoreType.DMA,
        pltpu.SemaphoreType.DMA((count,)),
    ]
    return call(spread_kernel, shape, [hbm()], hbm(), own, scratch_shapes=scratch)


def pick_kernel(rows_ref, *refs):
    out_refs, sems = refs[:4], refs[4]
    core, a, b, _, _, h = position()
    pairs = []
    for d, out_ref in enumerate(out_refs):
        for f in range(8):
            row, column = f >> 1, f & 1
            z = 4 * h + 2 * column + (b ^ (d & 1))
            y = 2 * row + (a ^ (d >> 1))
            z, y = (z + 8 - core) & 7, (y + 8 - core) & 7
            there = ((z & 3) * 8 + y) * 2 + (z >> 2)
            pairs.append((rows_ref.at[there], out_ref.at[f]))
    for copy in run_copies(pairs, sems):
        copy.wait()


def pick(rows):
    shape = pltpu.HBM((8,) + rows.shape[1:], rows.dtype)
    scratch = [pltpu.SemaphoreType.DMA((32,))]
    return call(pick_kernel, [shape] * 4, [vmem()], [hbm()] * 4, rows, scratch_shapes=scratch)


def gram_part(rows, x):
    whitened = lax.dot_general(rows, x, ROWS_ROWS, preferred_element_type=f32)
    return jnp.dot(whitened.astype(bf16), x, preferred_element_type=f32).astype(bf16)


def own_rows_kernel(rows_ref, out_ref):
    out_ref[...] = rows_ref[position()[5]]


def own_rows(rows):
    shape = jax.ShapeDtypeStruct(rows.shape[1:], bf16)
    return call(own_rows_kernel, shape, [vmem()], vmem(), rows)


def other_rows_kernel(rows_ref, x_ref, out_ref):
    out_ref[...] = rows_ref[1 - position()[5]]


def other_rows(rows, x):
    shape = jax.ShapeDtypeStruct(rows.shape[1:], bf16)
    return call(other_rows_kernel, shape, [vmem()] * 2, vmem(), rows, x)


def own_moment_kernel(rows_ref, x_ref, out_ref):
    out_ref[...] = gram_part(rows_ref[...], x_ref[...])


def own_moment(rows, x):
    shape = jax.ShapeDtypeStruct(rows.shape, bf16)
    return call(own_moment_kernel, shape, [vmem()] * 2, vmem(), rows, x)


def moment_kernel(rows_ref, x_ref, out_ref):
    out_ref[...] = gram_part(rows_ref[position()[5]], x_ref[...])


def moment_of(rows, x):
    shape = jax.ShapeDtypeStruct(rows.shape[1:], bf16)
    return call(moment_kernel, shape, [vmem()] * 2, vmem(), rows, x)


def join_kernel(*refs):
    moments, gradients, out_ref = refs[:4], refs[4:8], refs[8]
    for f in range(8):
        for first, parts in ((0, moments), (16, gradients)):
            total = parts[0][f].astype(f32)
            for part in parts[1:]:
                total = total + part[f].astype(f32)
            out_ref[f, first : first + 16] = total.astype(bf16)


def join(moments, gradients):
    width = gradients[0].shape[2]
    moments = [m.reshape(8, 16, width) for m in moments]
    shape = jax.ShapeDtypeStruct((8, 32, width), bf16)
    return call(join_kernel, shape, [vmem()] * 8, vmem(), *moments, *gradients)


def panel_kernel(tokens, sums_ref, own_ref, out_ref):
    total = sums_ref[0].astype(f32)
    for k in range(1, 8):
        total = total + sums_ref[k].astype(f32)
    inner_rows = total[:16] / tokens + damping * own_ref[...].astype(bf16).astype(f32)
    high = inner_rows.astype(bf16)
    low = (inner_rows - high.astype(f32)).astype(bf16)
    out_ref[...] = jnp.concatenate([high, low, total[16:].astype(bf16)], axis=0)


def panel(tokens, sums, own):
    shape = jax.ShapeDtypeStruct((48, own.shape[1]), bf16)
    kernel = functools.partial(panel_kernel, tokens)
    return call(kernel, shape, [vmem()] * 2, vmem(), sums, own)


def finish_kernel(left_ref, own_ref, *refs):
    blocks, new_ref, direction_ref, rows = refs[:-3], refs[-3], refs[-2], refs[-1]
    _, _, _, yh, zh, h = position()
    at = h * 128 + (2 * yh + zh) * 16
    own = own_ref[...]
    first = 0
    for block in blocks:
        rows[pl.ds(first, block.shape[0])] = block[...]
        first += block.shape[0]
    product = lax.dot_general(left_ref[...], rows[...], ROWS_ROWS, preferred_element_type=f32)
    curve = product[:16] + product[16:32]
    column = lax.broadcasted_iota(jnp.int32, curve.shape, 1)
    row = lax.broadcasted_iota(jnp.int32, curve.shape, 0)
    curve = curve - (column == row + at).astype(f32)
    right = jnp.concatenate([curve.astype(bf16), product[32:].astype(bf16)], axis=0)
    result = jnp.dot(right, rows[...], preferred_element_type=f32)
    new_ref[...] = own - 0.5 * step_size * result[:16]
    direction_ref[...] = result[16:]


def finish(left, own, blocks):
    width = own.shape[1]
    return call(
        finish_kernel,
        [jax.ShapeDtypeStruct(own.shape, f32)] * 2,
        [vmem()] * (2 + len(blocks)),
        [vmem()] * 2,
        left,
        own,
        *[block.reshape(-1, width) for block in blocks],
        scratch_shapes=[pltpu.VMEM((width, width), bf16)],
    )


def on_device(activations, cotangent, factor):
    seq_count = lax.axis_size(SEQ)
    owned = factor.shape[1]
    width = factor.shape[0]
    total_tokens = activations.shape[0] * seq_count

    def turn(block, pairs):
        return lax.ppermute(block, PLANES, pairs)

    own = factor.T
    mine = exchange(spread(own, 16), COSETS).reshape(2, 8 * owned, width)

    gradient_part = lax.dot_general(
        cotangent, activations, TOKENS_FIRST, preferred_element_type=f32
    ).astype(bf16)
    parts = pick(gradient_part.reshape(2 * seq_count, owned, width))
    gradients = [parts[0]]
    for d in (1, 2, 3):
        gradients.append(turn(parts[d], INNER[d]))

    own_block = own_rows(mine)
    near = {}
    for d in ORDER:
        near[d] = turn(own_block if d == 3 else mine, INNER[d])
    other_block = other_rows(mine, activations)
    moments = [own_moment(own_block, activations)]
    for d in ORDER:
        moment = (own_moment if d == 3 else moment_of)(near[d], activations)
        moments.append(turn(moment, INNER[d]))
    late = turn(other_block, INNER[3])
    joined = join(moments, gradients)
    sums = exchange(joined, FAR_GROUPS)

    left = panel(total_tokens, sums, own)
    new_factor, direction = finish(left, own, [mine, near[1], near[2], near[3], late])
    return (new_factor.T, direction.T)


def solution(mesh):
    torus = Mesh(
        mesh.devices.reshape(4, 8, mesh.shape["blk"], mesh.shape["grp"]),
        ("seq_0", "seq_1", "blk", "grp"),
    )
    return jax.shard_map(
        on_device,
        mesh=torus,
        in_specs=(P(SEQ, "blk"), P(SEQ, None), P("blk", SEQ_GRP)),
        out_specs=(P("blk", SEQ_GRP), P("blk", SEQ_GRP)),
        check_vma=False,
    )
```

profile of v0, /device:TPU:1, one launch (start us, length us, event | category | flops | bytes accessed | tf_op | source)
XLA Modules:
  0.0 109.3 jit_solution(10252117004888776827)
XLA Ops:
  0.6 0.0 copy-start
  0.6 0.0 copy-start.1
  0.7 1.9 %shard_map.50 = bf16[16,16,1024]{2,1,0:T(8,128)(2,1)} custom-call(f32[16,1024]{1,0:T(8,128)} %bitcast.23), custom_call_target="tpu_custom_call" | custom-call | tf_op jit(solution)/shard_map/pallas_call | solution.py:98
  2.6 34.1 %all_to_all.10 = bf16[16,16,1024]{2,1,0:T(8,128)(2,1)S(1)} all-to-all(bf16[16,16,1024]{2,1,0:T(8,128)(2,1)} %shard_map.50), channel_id=1, replica_groups={{0,256,32,288,64,320,96,352,1,257,33,289,65,321,97,353},{128,384,160,41..., dimensions={0} | all-to-all | bytes 1048576 | tf_op jit(solution)/shard_map/all_to_all | solution.py:70
  36.7 2.3 %collective-permute-start.2 = (bf16[2,128,1024]{2,1,0:T(8,128)(2,1)S(1)}, bf16[2,128,1024]{2,1,0:T(8,128)(2,1)S(1)}, u32[]{:S(2)}, u32[]{:S(2)}) collective-permute-start(bf16[2,128,1024]{2,1,0:T(8,128)(2,1)S(1)} %bitcast.15), channel_id=1, source_target_pairs={{0,16},{499,387},{4,20},{503,391},{8,24},{507,395},{12,28},{511,39... | collective-permute-start | bytes 1572872 | tf_op jit(solution)/shard_map/ppermute | solution.py:266
  39.0 3.0 %collective-permute-start.4 = (bf16[2,128,1024]{2,1,0:T(8,128)(2,1)S(1)}, bf16[2,128,1024]{2,1,0:T(8,128)(2,1)S(1)}, u32[]{:S(2)}, u32[]{:S(2)}) collective-permute-start(bf16[2,128,1024]{2,1,0:T(8,128)(2,1)S(1)} %bitcast.16), channel_id=1, source_target_pairs={{0,128},{499,114},{4,132},{503,118},{8,136},{507,122},{12,140},{51... | collective-permute-start | bytes 1572872 | tf_op jit(solution)/shard_map/ppermute | solution.py:266
  42.0 5.5 %collective-permute-start = (bf16[128,1024]{1,0:T(8,128)(2,1)S(1)}, bf16[128,1024]{1,0:T(8,128)(2,1)S(1)}, u32[]{:S(2)}, u32[]{:S(2)}) collective-permute-start(bf16[128,1024]{1,0:T(8,128)(2,1)S(1)} %shard_map.51.rows_ref), channel_id=1, source_target_pairs={{0,144},{499,2},{4,148},{503,6},{8,152},{507,10},{12,156},{511,14}... | collective-permute-start | bytes 786440 | tf_op jit(solution)/shard_map/ppermute | solution.py:266
  47.5 2.4 %convolution_convert_fusion = bf16[1024,1024]{1,0:T(8,128)(2,1)S(1)} fusion(bf16[1024,1024]{1,0:T(8,128)(2,1)S(1)} %copy-done, bf16[1024,1024]{1,0:T(8,128)(2,1)S(1)} %copy-done.1), kind=kOutput, calls=%fused_computation | convolution fusion | flops 2148532224 | bytes 6291456 | tf_op jit(solution)/shard_map/dot_general | solution.py:271
  50.0 1.3 %shard_map.56 = (bf16[8,16,1024]{2,1,0:T(8,128)(2,1)}, bf16[8,16,1024]{2,1,0:T(8,128)(2,1)}, bf16[8,16,1024]{2,1,0:T(8,128)(2,1)}, bf16[8,16,1024]{2,1,0:T(8,128)(2,1)}) custom-call(bf16[64,16,1024]{2,1,0:T(8,128)(2,1)S(1)} %bitcast.19), custom_call_target="tpu_custom_call" | custom-call | tf_op jit(solution)/shard_map/pallas_call | solution.py:98
  51.3 3.3 %collective-permute-start.6 = (bf16[8,16,1024]{2,1,0:T(8,128)(2,1)}, bf16[8,16,1024]{2,1,0:T(8,128)(2,1)S(1)}, u32[]{:S(2)}, u32[]{:S(2)}) collective-permute-start(bf16[8,16,1024]{2,1,0:T(8,128)(2,1)} %get-tuple-element.9), channel_id=1, source_target_pairs={{0,128},{499,114},{4,132},{503,118},{8,136},{507,122},{12,140},{51... | collective-permute-start | bytes 786440 | tf_op jit(solution)/shard_map/ppermute | solution.py:266
  54.6 1.9 %collective-permute-start.7 = (bf16[8,16,1024]{2,1,0:T(8,128)(2,1)}, bf16[8,16,1024]{2,1,0:T(8,128)(2,1)S(1)}, u32[]{:S(2)}, u32[]{:S(2)}) collective-permute-start(bf16[8,16,1024]{2,1,0:T(8,128)(2,1)} %get-tuple-element.10), channel_id=1, source_target_pairs={{0,16},{499,387},{4,20},{503,391},{8,24},{507,395},{12,28},{511,39... | collective-permute-start | bytes 786440 | tf_op jit(solution)/shard_map/ppermute | solution.py:266
  56.6 0.0 collective-permute-done.rows_ref.refs_3_
  56.6 5.5 %collective-permute-start.8 = (bf16[8,16,1024]{2,1,0:T(8,128)(2,1)}, bf16[8,16,1024]{2,1,0:T(8,128)(2,1)S(1)}, u32[]{:S(2)}, u32[]{:S(2)}) collective-permute-start(bf16[8,16,1024]{2,1,0:T(8,128)(2,1)} %get-tuple-element.11), channel_id=1, source_target_pairs={{0,144},{499,2},{4,148},{503,6},{8,152},{507,10},{12,156},{511,14}... | collective-permute-start | bytes 786440 | tf_op jit(solution)/shard_map/ppermute | solution.py:266
  62.1 1.1 %shard_map.53 = bf16[128,1024]{1,0:T(8,128)(2,1)S(1)} custom-call(bf16[128,1024]{1,0:T(8,128)(2,1)S(1)} %collective-permute-done.rows_ref.refs_3_, bf16[1024,1024]{1,0:T(8,128)(2,1)S(1)} %copy-done.1), custom_call_target="tpu_custom_call" | custom-call | tf_op jit(solution)/shard_map/pallas_call | solution.py:98
  63.2 3.1 %collective-permute-start.1 = (bf16[128,1024]{1,0:T(8,128)(2,1)S(1)}, bf16[128,1024]{1,0:T(8,128)(2,1)S(1)}, u32[]{:S(2)}, u32[]{:S(2)}) collective-permute-start(bf16[128,1024]{1,0:T(8,128)(2,1)S(1)} %shard_map.53), channel_id=1, source_target_pairs={{0,144},{499,2},{4,148},{503,6},{8,152},{507,10},{12,156},{511,14}... | collective-permute-start | bytes 786440 | tf_op jit(solution)/shard_map/ppermute | solution.py:266
  66.3 1.1 %shard_map.54 = bf16[128,1024]{1,0:T(8,128)(2,1)S(1)} custom-call(bf16[2,128,1024]{2,1,0:T(8,128)(2,1)S(1)} %collective-permute-done.2.rows_ref, bf16[1024,1024]{1,0:T(8,128)(2,1)S(1)} %copy-done.1), custom_call_target="tpu_custom_call" | custom-call | tf_op jit(solution)/shard_map/pallas_call | solution.py:98
  67.5 4.7 %collective-permute-start.3 = (bf16[128,1024]{1,0:T(8,128)(2,1)S(1)}, bf16[128,1024]{1,0:T(8,128)(2,1)S(1)}, u32[]{:S(2)}, u32[]{:S(2)}) collective-permute-start(bf16[128,1024]{1,0:T(8,128)(2,1)S(1)} %shard_map.54), channel_id=1, source_target_pairs={{0,16},{499,387},{4,20},{503,391},{8,24},{507,395},{12,28},{511,39... | collective-permute-start | bytes 786440 | tf_op jit(solution)/shard_map/ppermute | solution.py:266
  72.1 1.1 %shard_map.55 = bf16[128,1024]{1,0:T(8,128)(2,1)S(1)} custom-call(bf16[2,128,1024]{2,1,0:T(8,128)(2,1)S(1)} %collective-permute-done.4.rows_ref, bf16[1024,1024]{1,0:T(8,128)(2,1)S(1)} %copy-done.1), custom_call_target="tpu_custom_call" | custom-call | tf_op jit(solution)/shard_map/pallas_call | solution.py:98
  73.3 3.2 %collective-permute-start.5 = (bf16[128,1024]{1,0:T(8,128)(2,1)S(1)}, bf16[128,1024]{1,0:T(8,128)(2,1)S(1)}, u32[]{:S(2)}, u32[]{:S(2)}) collective-permute-start(bf16[128,1024]{1,0:T(8,128)(2,1)S(1)} %shard_map.55), channel_id=1, source_target_pairs={{0,128},{499,114},{4,132},{503,118},{8,136},{507,122},{12,140},{51... | collective-permute-start | bytes 786440 | tf_op jit(solution)/shard_map/ppermute | solution.py:266
  76.5 1.1 %shard_map.52 = bf16[128,1024]{1,0:T(8,128)(2,1)S(1)} custom-call(bf16[128,1024]{1,0:T(8,128)(2,1)S(1)} %shard_map.51.rows_ref, bf16[1024,1024]{1,0:T(8,128)(2,1)S(1)} %copy-done.1), custom_call_target="tpu_custom_call" | custom-call | tf_op jit(solution)/shard_map/pallas_call | solution.py:98
  77.6 4.0 %collective-permute-done.5 = bf16[128,1024]{1,0:T(8,128)(2,1)S(1)} collective-permute-done((bf16[128,1024]{1,0:T(8,128)(2,1)S(1)}, bf16[128,1024]{1,0:T(8,128)(2,1)S(1)}, u32[]{:S(2)}, u32[]{:S(2)}) %collective-permute-start.5) | collective-permute-done | bytes 262176 | tf_op jit(solution)/shard_map/ppermute | solution.py:266
  81.6 1.1 shard_map.57
  82.7 4.3 %all-to-all-start.1 = ((bf16[8,32,1024]{2,1,0:T(8,128)(2,1)}), bf16[8,32,1024]{2,1,0:T(8,128)(2,1)}, u32[]{:S(2)}, u32[]{:S(2)}) async-start(bf16[8,32,1024]{2,1,0:T(8,128)(2,1)} %shard_map.57), calls=%async_computation.1 | async-start | bytes 1048576 | tf_op jit(solution)/shard_map/all_to_all | solution.py:70
  87.0 0.0 copy-start.2
  87.0 1.6 %copy-done.2 = bf16[1024,1024]{1,0:T(8,128)(2,1)S(1)} copy-done((bf16[1024,1024]{1,0:T(8,128)(2,1)S(1)}, bf16[1024,1024]{1,0:T(8,128)(2,1)}, u32[]{:S(2)}) %copy-start.2) | copy-done | bytes 2097176
  88.6 0.7 shard_map.59
  89.3 3.2 %collective-permute-start.9 = (bf16[128,1024]{1,0:T(8,128)(2,1)}, bf16[128,1024]{1,0:T(8,128)(2,1)}, u32[]{:S(2)}, u32[]{:S(2)}) collective-permute-start(bf16[128,1024]{1,0:T(8,128)(2,1)} %shard_map.59), channel_id=1, source_target_pairs={{0,144},{499,2},{4,148},{503,6},{8,152},{507,10},{12,156},{511,14}... | collective-permute-start | bytes 786440 | tf_op jit(solution)/shard_map/ppermute | solution.py:266
  92.5 11.1 %all-to-all-done.1.sums_ref = bf16[8,32,1024]{2,1,0:T(8,128)(2,1)} async-done(((bf16[8,32,1024]{2,1,0:T(8,128)(2,1)}), bf16[8,32,1024]{2,1,0:T(8,128)(2,1)}, u32[]{:S(2)}, u32[]{:S(2)}) %all-to-all-start.1) | async-done | bytes 524320 | tf_op jit(solution)/shard_map/all_to_all | solution.py:70
  103.6 1.1 %shard_map.58.left_ref = bf16[48,1024]{1,0:T(8,128)(2,1)S(1)} custom-call(bf16[8,32,1024]{2,1,0:T(8,128)(2,1)} %all-to-all-done.1.sums_ref, f32[16,1024]{1,0:T(8,128)S(1)} %bitcast.24), custom_call_target="tpu_custom_call" | custom-call | tf_op jit(solution)/shard_map/pallas_call | solution.py:98
  104.8 0.8 collective-permute-done.9.refs_4_
  105.6 1.0 copy-done.4
  106.6 2.7 %shard_map.60 = (f32[16,1024]{1,0:T(8,128)}, f32[16,1024]{1,0:T(8,128)}) custom-call(bf16[48,1024]{1,0:T(8,128)(2,1)S(1)} %shard_map.58.left_ref, f32[16,1024]{1,0:T(8,128)S(1)} %bitcast.25, bf16[256,1024]{1,0:T(8,128)(2,1)S(1)} %bitcast.18, bf16[256,1024]{1,0:T(8,128)(2,1)S(1)} %bitcast.21, bf16[256,1024]{1,0:T(8,128)(2,1)S(1)} %bitcast.20, ...), custom_call_target="tpu_custom_call" | custom-call | tf_op jit(solution)/shard_map/pallas_call | solution.py:98
  (17 shorter events, 0.1 us)
Async XLA Ops:
  0.6 46.9 %copy-start = (bf16[1024,1024]{1,0:T(8,128)(2,1)S(1)}, bf16[1024,1024]{1,0:T(8,128)(2,1)}, u32[]{:S(2)}) copy-start(bf16[1024,1024]{1,0:T(8,128)(2,1)} %param.4) | copy-start | bytes 6291460
  0.6 46.9 %copy-start.1 = (bf16[1024,1024]{1,0:T(8,128)(2,1)S(1)}, bf16[1024,1024]{1,0:T(8,128)(2,1)}, u32[]{:S(2)}) copy-start(bf16[1024,1024]{1,0:T(8,128)(2,1)} %x_ref.9) | copy-start | bytes 6291460
  36.7 26.5 %collective-permute-start.2 = (bf16[2,128,1024]{2,1,0:T(8,128)(2,1)S(1)}, bf16[2,128,1024]{2,1,0:T(8,128)(2,1)S(1)}, u32[]{:S(2)}, u32[]{:S(2)}) collective-permute-start(bf16[2,128,1024]{2,1,0:T(8,128)(2,1)S(1)} %bitcast.15), channel_id=1, source_target_pairs={{0,16},{499,387},{4,20},{503,391},{8,24},{507,395},{12,28},{511,39... | collective-permute-start | bytes 1572872 | tf_op jit(solution)/shard_map/ppermute | solution.py:266
  39.0 28.5 %collective-permute-start.4 = (bf16[2,128,1024]{2,1,0:T(8,128)(2,1)S(1)}, bf16[2,128,1024]{2,1,0:T(8,128)(2,1)S(1)}, u32[]{:S(2)}, u32[]{:S(2)}) collective-permute-start(bf16[2,128,1024]{2,1,0:T(8,128)(2,1)S(1)} %bitcast.16), channel_id=1, source_target_pairs={{0,128},{499,114},{4,132},{503,118},{8,136},{507,122},{12,140},{51... | collective-permute-start | bytes 1572872 | tf_op jit(solution)/shard_map/ppermute | solution.py:266
  42.0 14.6 %collective-permute-start = (bf16[128,1024]{1,0:T(8,128)(2,1)S(1)}, bf16[128,1024]{1,0:T(8,128)(2,1)S(1)}, u32[]{:S(2)}, u32[]{:S(2)}) collective-permute-start(bf16[128,1024]{1,0:T(8,128)(2,1)S(1)} %shard_map.51.rows_ref), channel_id=1, source_target_pairs={{0,144},{499,2},{4,148},{503,6},{8,152},{507,10},{12,156},{511,14}... | collective-permute-start | bytes 786440 | tf_op jit(solution)/shard_map/ppermute | solution.py:266
  51.3 22.0 %collective-permute-start.6 = (bf16[8,16,1024]{2,1,0:T(8,128)(2,1)}, bf16[8,16,1024]{2,1,0:T(8,128)(2,1)S(1)}, u32[]{:S(2)}, u32[]{:S(2)}) collective-permute-start(bf16[8,16,1024]{2,1,0:T(8,128)(2,1)} %get-tuple-element.9), channel_id=1, source_target_pairs={{0,128},{499,114},{4,132},{503,118},{8,136},{507,122},{12,140},{51... | collective-permute-start | bytes 786440 | tf_op jit(solution)/shard_map/ppermute | solution.py:266
  54.6 23.0 %collective-permute-start.7 = (bf16[8,16,1024]{2,1,0:T(8,128)(2,1)}, bf16[8,16,1024]{2,1,0:T(8,128)(2,1)S(1)}, u32[]{:S(2)}, u32[]{:S(2)}) collective-permute-start(bf16[8,16,1024]{2,1,0:T(8,128)(2,1)} %get-tuple-element.10), channel_id=1, source_target_pairs={{0,16},{499,387},{4,20},{503,391},{8,24},{507,395},{12,28},{511,39... | collective-permute-start | bytes 786440 | tf_op jit(solution)/shard_map/ppermute | solution.py:266
  56.6 21.0 %collective-permute-start.8 = (bf16[8,16,1024]{2,1,0:T(8,128)(2,1)}, bf16[8,16,1024]{2,1,0:T(8,128)(2,1)S(1)}, u32[]{:S(2)}, u32[]{:S(2)}) collective-permute-start(bf16[8,16,1024]{2,1,0:T(8,128)(2,1)} %get-tuple-element.11), channel_id=1, source_target_pairs={{0,144},{499,2},{4,148},{503,6},{8,152},{507,10},{12,156},{511,14}... | collective-permute-start | bytes 786440 | tf_op jit(solution)/shard_map/ppermute | solution.py:266
  63.2 14.4 %collective-permute-start.1 = (bf16[128,1024]{1,0:T(8,128)(2,1)S(1)}, bf16[128,1024]{1,0:T(8,128)(2,1)S(1)}, u32[]{:S(2)}, u32[]{:S(2)}) collective-permute-start(bf16[128,1024]{1,0:T(8,128)(2,1)S(1)} %shard_map.53), channel_id=1, source_target_pairs={{0,144},{499,2},{4,148},{503,6},{8,152},{507,10},{12,156},{511,14}... | collective-permute-start | bytes 786440 | tf_op jit(solution)/shard_map/ppermute | solution.py:266
  67.4 14.2 %copy-start.6 = (bf16[8,16,1024]{2,1,0:T(8,128)(2,1)S(1)}, bf16[8,16,1024]{2,1,0:T(8,128)(2,1)}, u32[]{:S(2)}) copy-start(bf16[8,16,1024]{2,1,0:T(8,128)(2,1)} %get-tuple-element.8.refs_4_) | copy-start | bytes 786436
  67.5 10.1 %copy-start.3 = (bf16[2,128,1024]{2,1,0:T(8,128)(2,1)}, bf16[2,128,1024]{2,1,0:T(8,128)(2,1)S(1)}, u32[]{:S(2)}) copy-start(bf16[2,128,1024]{2,1,0:T(8,128)(2,1)S(1)} %collective-permute-done.4.rows_ref) | copy-start | bytes 1572868
  67.5 10.2 %collective-permute-start.3 = (bf16[128,1024]{1,0:T(8,128)(2,1)S(1)}, bf16[128,1024]{1,0:T(8,128)(2,1)S(1)}, u32[]{:S(2)}, u32[]{:S(2)}) collective-permute-start(bf16[128,1024]{1,0:T(8,128)(2,1)S(1)} %shard_map.54), channel_id=1, source_target_pairs={{0,16},{499,387},{4,20},{503,391},{8,24},{507,395},{12,28},{511,39... | collective-permute-start | bytes 786440 | tf_op jit(solution)/shard_map/ppermute | solution.py:266
  73.3 8.3 %collective-permute-start.5 = (bf16[128,1024]{1,0:T(8,128)(2,1)S(1)}, bf16[128,1024]{1,0:T(8,128)(2,1)S(1)}, u32[]{:S(2)}, u32[]{:S(2)}) collective-permute-start(bf16[128,1024]{1,0:T(8,128)(2,1)S(1)} %shard_map.55), channel_id=1, source_target_pairs={{0,128},{499,114},{4,132},{503,118},{8,136},{507,122},{12,140},{51... | collective-permute-start | bytes 786440 | tf_op jit(solution)/shard_map/ppermute | solution.py:266
  82.7 21.0 %copy-start.5 = (f32[1024,16]{0,1:T(8,128)S(1)}, f32[1024,16]{0,1:T(8,128)}, u32[]{:S(2)}) copy-start(f32[1024,16]{0,1:T(8,128)} %param.5) | copy-start | bytes 196612
  82.7 21.0 %all-to-all-start.1 = ((bf16[8,32,1024]{2,1,0:T(8,128)(2,1)}), bf16[8,32,1024]{2,1,0:T(8,128)(2,1)}, u32[]{:S(2)}, u32[]{:S(2)}) async-start(bf16[8,32,1024]{2,1,0:T(8,128)(2,1)} %shard_map.57), calls=%async_computation.1 | async-start | bytes 1048576 | tf_op jit(solution)/shard_map/all_to_all | solution.py:70
  87.0 1.6 %copy-start.2 = (bf16[1024,1024]{1,0:T(8,128)(2,1)S(1)}, bf16[1024,1024]{1,0:T(8,128)(2,1)}, u32[]{:S(2)}) copy-start(bf16[1024,1024]{1,0:T(8,128)(2,1)} %x_ref.9) | copy-start | bytes 6291460
  89.3 16.3 %collective-permute-start.9 = (bf16[128,1024]{1,0:T(8,128)(2,1)}, bf16[128,1024]{1,0:T(8,128)(2,1)}, u32[]{:S(2)}, u32[]{:S(2)}) collective-permute-start(bf16[128,1024]{1,0:T(8,128)(2,1)} %shard_map.59), channel_id=1, source_target_pairs={{0,144},{499,2},{4,148},{503,6},{8,152},{507,10},{12,156},{511,14}... | collective-permute-start | bytes 786440 | tf_op jit(solution)/shard_map/ppermute | solution.py:266
  105.6 1.0 copy-start.4
where the time goes:
time: 110 us; the launch traced here: 109 us
  starting transfers between devices  40 us (36%)
  blocking collectives  34.1 us (31%)
  waiting for transfers between devices  15.9 us (14%)
  Pallas kernels  13.3 us (12%)
  local copies, waits for them, and re-layouts  2.66 us (2%)
  matrix products  2.41 us (2%)
    ppermute x10, starting transfers between devices, turn(): return lax.ppermute(block, PLANES, pairs)  35.7 us
    all_to_all x1, blocking collectives, exchange(): lax.all_to_all(blocks, PLANES, split_axis=0, concat_axis=0, tiled=True, a...  34.1 us
    pallas_call x11, Pallas kernels, call(): pl.pallas_call(kernel, out_shape=out_shape, in_specs=in_specs, out_specs=...  13.3 us
    all_to_all x1, waiting for transfers between devices, exchange(): lax.all_to_all(blocks, PLANES, split_axis=0, concat_axis=0, tiled=True, a...  11.1 us
    ppermute x10, waiting for transfers between devices, turn(): return lax.ppermute(block, PLANES, pairs)  4.82 us
    all_to_all x1, starting transfers between devices, exchange(): lax.all_to_all(blocks, PLANES, split_axis=0, concat_axis=0, tiled=True, a...  4.28 us
    unnamed x14, local copies, waits for them, and re-layouts  2.66 us
    dot_general x1, matrix products, on_device(): lax.dot_general(cotangent, activations, TOKENS_FIRST, preferred_element_t...  2.41 us
  transfers between devices with their start and end apart: 11, of which 3 were waited for; matrix products, arithmetic and copies ran while one was open for 2% of the time, Pallas kernels for 7%

commit v1 on v0

--- a/solution.py
+++ b/solution.py
@@ -171,13 +171,20 @@
     return call(other_rows_kernel, shape, [vmem()] * 2, vmem(), rows, x)
 
 
-def own_moment_kernel(rows_ref, x_ref, out_ref):
-    out_ref[...] = gram_part(rows_ref[...], x_ref[...])
-
-
-def own_moment(rows, x):
+def pair_kernel(own_ref, rows_ref, x_ref, own_out_ref, out_ref, both):
+    both[:128] = own_ref[...]
+    both[128:] = rows_ref[...]
+    total = gram_part(both[...], x_ref[...])
+    own_out_ref[...] = total[:128]
+    out_ref[...] = total[128:]
+
+
+def moment_pair(own, rows, x):
     shape = jax.ShapeDtypeStruct(rows.shape, bf16)
-    return call(own_moment_kernel, shape, [vmem()] * 2, vmem(), rows, x)
+    scratch = [pltpu.VMEM((256, x.shape[1]), bf16)]
+    return call(
+        pair_kernel, [shape] * 2, [vmem()] * 3, [vmem()] * 2, own, rows, x, scratch_shapes=scratch
+    )
 
 
 def moment_kernel(rows_ref, x_ref, out_ref):
@@ -281,9 +288,13 @@
     for d in ORDER:
         near[d] = turn(own_block if d == 3 else mine, INNER[d])
     other_block = other_rows(mine, activations)
-    moments = [own_moment(own_block, activations)]
+    moments = []
     for d in ORDER:
-        moment = (own_moment if d == 3 else moment_of)(near[d], activations)
+        if d == 3:
+            own_part, moment = moment_pair(own_block, near[d], activations)
+            moments.append(own_part)
+        else:
+            moment = moment_of(near[d], activations)
         moments.append(turn(moment, INNER[d]))
     late = turn(other_block, INNER[3])
     joined = join(moments, gradients)

time: 110 us -> 110 us (level)
  waiting for transfers between devices: 15.9 us -> 17.1 us
    ppermute x10, waiting for transfers between devices: 4.82 us -> 5.95 us  [turn(): return lax.ppermute(block, PLANES, pairs)]
    pallas_call x11 -> x10, Pallas kernels: 13.3 us -> 12.4 us  [call(): pl.pallas_call(kernel, out_shape=out_shape, in_specs=in_specs, out_specs=...]
  transfers between devices with their start and end apart: 11 -> 11, of which waited for: 3 -> 3; matrix products, arithmetic and copies ran while one was open for 2% -> 2% of each run, Pallas kernels for 7% -> 6%
where the time goes in v1:
time: 110 us
  starting transfers between devices  40 us (36%)
  blocking collectives  34.1 us (31%)
  waiting for transfers between devices  17.1 us (16%)
  Pallas kernels  12.4 us (11%)
  local copies, waits for them, and re-layouts  2.66 us (2%)
  matrix products  2.41 us (2%)
    ppermute x10, starting transfers between devices, turn(): return lax.ppermute(block, PLANES, pairs)  35.8 us
    all_to_all x1, blocking collectives, exchange(): lax.all_to_all(blocks, PLANES, split_axis=0, concat_axis=0, tiled=True, a...  34.1 us
    pallas_call x10, Pallas kernels, call(): pl.pallas_call(kernel, out_shape=out_shape, in_specs=in_specs, out_specs=...  12.4 us
    all_to_all x1, waiting for transfers between devices, exchange(): lax.all_to_all(blocks, PLANES, split_axis=0, concat_axis=0, tiled=True, a...  11.1 us
    ppermute x10, waiting for transfers between devices, turn(): return lax.ppermute(block, PLANES, pairs)  5.95 us
    all_to_all x1, starting transfers between devices, exchange(): lax.all_to_all(blocks, PLANES, split_axis=0, concat_axis=0, tiled=True, a...  4.28 us
    unnamed x14, local copies, waits for them, and re-layouts  2.66 us
    dot_general x1, matrix products, on_device(): lax.dot_general(cotangent, activations, TOKENS_FIRST, preferred_element_t...  2.41 us
  transfers between devices with their start and end apart: 11, of which 3 were waited for; matrix products, arithmetic and copies ran while one was open for 2% of the time, Pallas kernels for 6%

profile of v1, /device:TPU:1, one launch (start us, length us, event | category | flops | bytes accessed | tf_op | source)
XLA Modules:
  0.0 109.5 jit_solution(6817014048913683381)
XLA Ops:
  0.6 0.0 copy-start
  0.6 0.0 copy-start.1
  0.7 2.0 %shard_map.50 = bf16[16,16,1024]{2,1,0:T(8,128)(2,1)} custom-call(f32[16,1024]{1,0:T(8,128)} %bitcast.22), custom_call_target="tpu_custom_call" | custom-call | tf_op jit(solution)/shard_map/pallas_call | solution.py:98
  2.6 34.1 %all_to_all.10 = bf16[16,16,1024]{2,1,0:T(8,128)(2,1)S(1)} all-to-all(bf16[16,16,1024]{2,1,0:T(8,128)(2,1)} %shard_map.50), channel_id=1, replica_groups={{0,256,32,288,64,320,96,352,1,257,33,289,65,321,97,353},{128,384,160,41..., dimensions={0} | all-to-all | bytes 1048576 | tf_op jit(solution)/shard_map/all_to_all | solution.py:70
  36.7 2.3 %collective-permute-start.2 = (bf16[2,128,1024]{2,1,0:T(8,128)(2,1)S(1)}, bf16[2,128,1024]{2,1,0:T(8,128)(2,1)S(1)}, u32[]{:S(2)}, u32[]{:S(2)}) collective-permute-start(bf16[2,128,1024]{2,1,0:T(8,128)(2,1)S(1)} %bitcast.15), channel_id=1, source_target_pairs={{0,16},{499,387},{4,20},{503,391},{8,24},{507,395},{12,28},{511,39... | collective-permute-start | bytes 1572872 | tf_op jit(solution)/shard_map/ppermute | solution.py:273
  39.0 3.0 %collective-permute-start.4 = (bf16[2,128,1024]{2,1,0:T(8,128)(2,1)S(1)}, bf16[2,128,1024]{2,1,0:T(8,128)(2,1)S(1)}, u32[]{:S(2)}, u32[]{:S(2)}) collective-permute-start(bf16[2,128,1024]{2,1,0:T(8,128)(2,1)S(1)} %bitcast.16), channel_id=1, source_target_pairs={{0,128},{499,114},{4,132},{503,118},{8,136},{507,122},{12,140},{51... | collective-permute-start | bytes 1572872 | tf_op jit(solution)/shard_map/ppermute | solution.py:273
  42.0 5.5 %collective-permute-start = (bf16[128,1024]{1,0:T(8,128)(2,1)S(1)}, bf16[128,1024]{1,0:T(8,128)(2,1)S(1)}, u32[]{:S(2)}, u32[]{:S(2)}) collective-permute-start(bf16[128,1024]{1,0:T(8,128)(2,1)S(1)} %shard_map.51.own_ref), channel_id=1, source_target_pairs={{0,144},{499,2},{4,148},{503,6},{8,152},{507,10},{12,156},{511,14}... | collective-permute-start | bytes 786440 | tf_op jit(solution)/shard_map/ppermute | solution.py:273
  47.5 2.4 %convolution_convert_fusion = bf16[1024,1024]{1,0:T(8,128)(2,1)S(1)} fusion(bf16[1024,1024]{1,0:T(8,128)(2,1)S(1)} %copy-done, bf16[1024,1024]{1,0:T(8,128)(2,1)S(1)} %copy-done.1), kind=kOutput, calls=%fused_computation | convolution fusion | flops 2148532224 | bytes 6291456 | tf_op jit(solution)/shard_map/dot_general | solution.py:278
  50.0 1.3 %shard_map.55 = (bf16[8,16,1024]{2,1,0:T(8,128)(2,1)}, bf16[8,16,1024]{2,1,0:T(8,128)(2,1)}, bf16[8,16,1024]{2,1,0:T(8,128)(2,1)}, bf16[8,16,1024]{2,1,0:T(8,128)(2,1)}) custom-call(bf16[64,16,1024]{2,1,0:T(8,128)(2,1)S(1)} %bitcast.19), custom_call_target="tpu_custom_call" | custom-call | tf_op jit(solution)/shard_map/pallas_call | solution.py:98
  51.3 3.3 %collective-permute-start.6 = (bf16[8,16,1024]{2,1,0:T(8,128)(2,1)}, bf16[8,16,1024]{2,1,0:T(8,128)(2,1)S(1)}, u32[]{:S(2)}, u32[]{:S(2)}) collective-permute-start(bf16[8,16,1024]{2,1,0:T(8,128)(2,1)} %get-tuple-element.13), channel_id=1, source_target_pairs={{0,128},{499,114},{4,132},{503,118},{8,136},{507,122},{12,140},{51... | collective-permute-start | bytes 786440 | tf_op jit(solution)/shard_map/ppermute | solution.py:273
  54.6 1.9 %collective-permute-start.7 = (bf16[8,16,1024]{2,1,0:T(8,128)(2,1)}, bf16[8,16,1024]{2,1,0:T(8,128)(2,1)S(1)}, u32[]{:S(2)}, u32[]{:S(2)}) collective-permute-start(bf16[8,16,1024]{2,1,0:T(8,128)(2,1)} %get-tuple-element.14), channel_id=1, source_target_pairs={{0,16},{499,387},{4,20},{503,391},{8,24},{507,395},{12,28},{511,39... | collective-permute-start | bytes 786440 | tf_op jit(solution)/shard_map/ppermute | solution.py:273
  56.6 0.0 collective-permute-done.rows_ref.refs_3_
  56.6 5.5 %collective-permute-start.8 = (bf16[8,16,1024]{2,1,0:T(8,128)(2,1)}, bf16[8,16,1024]{2,1,0:T(8,128)(2,1)S(1)}, u32[]{:S(2)}, u32[]{:S(2)}) collective-permute-start(bf16[8,16,1024]{2,1,0:T(8,128)(2,1)} %get-tuple-element.15), channel_id=1, source_target_pairs={{0,144},{499,2},{4,148},{503,6},{8,152},{507,10},{12,156},{511,14}... | collective-permute-start | bytes 786440 | tf_op jit(solution)/shard_map/ppermute | solution.py:273
  62.1 1.3 %shard_map.52 = (bf16[128,1024]{1,0:T(8,128)(2,1)S(1)}, bf16[128,1024]{1,0:T(8,128)(2,1)S(1)}) custom-call(bf16[128,1024]{1,0:T(8,128)(2,1)S(1)} %shard_map.51.own_ref, bf16[128,1024]{1,0:T(8,128)(2,1)S(1)} %collective-permute-done.rows_ref.refs_3_, bf16[1024,1024]{1,0:T(8,128)(2,1)S(1)} %copy-done.1), custom_call_target="tpu_custom_call" | custom-call | tf_op jit(solution)/shard_map/pallas_call | solution.py:98
  63.4 0.0 collective-permute-done.2.rows_ref
  63.4 3.1 %collective-permute-start.1 = (bf16[128,1024]{1,0:T(8,128)(2,1)S(1)}, bf16[128,1024]{1,0:T(8,128)(2,1)S(1)}, u32[]{:S(2)}, u32[]{:S(2)}) collective-permute-start(bf16[128,1024]{1,0:T(8,128)(2,1)S(1)} %get-tuple-element.11), channel_id=1, source_target_pairs={{0,144},{499,2},{4,148},{503,6},{8,152},{507,10},{12,156},{511,14}... | collective-permute-start | bytes 786440 | tf_op jit(solution)/shard_map/ppermute | solution.py:273
  66.5 1.1 %shard_map.53 = bf16[128,1024]{1,0:T(8,128)(2,1)S(1)} custom-call(bf16[2,128,1024]{2,1,0:T(8,128)(2,1)S(1)} %collective-permute-done.2.rows_ref, bf16[1024,1024]{1,0:T(8,128)(2,1)S(1)} %copy-done.1), custom_call_target="tpu_custom_call" | custom-call | tf_op jit(solution)/shard_map/pallas_call | solution.py:98
  67.7 4.7 %collective-permute-start.3 = (bf16[128,1024]{1,0:T(8,128)(2,1)S(1)}, bf16[128,1024]{1,0:T(8,128)(2,1)S(1)}, u32[]{:S(2)}, u32[]{:S(2)}) collective-permute-start(bf16[128,1024]{1,0:T(8,128)(2,1)S(1)} %shard_map.53), channel_id=1, source_target_pairs={{0,16},{499,387},{4,20},{503,391},{8,24},{507,395},{12,28},{511,39... | collective-permute-start | bytes 786440 | tf_op jit(solution)/shard_map/ppermute | solution.py:273
  72.3 1.1 %shard_map.54 = bf16[128,1024]{1,0:T(8,128)(2,1)S(1)} custom-call(bf16[2,128,1024]{2,1,0:T(8,128)(2,1)S(1)} %collective-permute-done.4.rows_ref, bf16[1024,1024]{1,0:T(8,128)(2,1)S(1)} %copy-done.1), custom_call_target="tpu_custom_call" | custom-call | tf_op jit(solution)/shard_map/pallas_call | solution.py:98
  73.5 3.2 %collective-permute-start.5 = (bf16[128,1024]{1,0:T(8,128)(2,1)S(1)}, bf16[128,1024]{1,0:T(8,128)(2,1)S(1)}, u32[]{:S(2)}, u32[]{:S(2)}) collective-permute-start(bf16[128,1024]{1,0:T(8,128)(2,1)S(1)} %shard_map.54), channel_id=1, source_target_pairs={{0,128},{499,114},{4,132},{503,118},{8,136},{507,122},{12,140},{51... | collective-permute-start | bytes 786440 | tf_op jit(solution)/shard_map/ppermute | solution.py:273
  76.7 5.1 %collective-permute-done.5 = bf16[128,1024]{1,0:T(8,128)(2,1)S(1)} collective-permute-done((bf16[128,1024]{1,0:T(8,128)(2,1)S(1)}, bf16[128,1024]{1,0:T(8,128)(2,1)S(1)}, u32[]{:S(2)}, u32[]{:S(2)}) %collective-permute-start.5) | collective-permute-done | bytes 262176 | tf_op jit(solution)/shard_map/ppermute | solution.py:273
  81.8 1.1 shard_map.56
  82.9 4.3 %all-to-all-start.1 = ((bf16[8,32,1024]{2,1,0:T(8,128)(2,1)}), bf16[8,32,1024]{2,1,0:T(8,128)(2,1)}, u32[]{:S(2)}, u32[]{:S(2)}) async-start(bf16[8,32,1024]{2,1,0:T(8,128)(2,1)} %shard_map.56), calls=%async_computation.1 | async-start | bytes 1048576 | tf_op jit(solution)/shard_map/all_to_all | solution.py:70
  87.2 0.0 copy-start.2
  87.2 1.6 %copy-done.2 = bf16[1024,1024]{1,0:T(8,128)(2,1)S(1)} copy-done((bf16[1024,1024]{1,0:T(8,128)(2,1)S(1)}, bf16[1024,1024]{1,0:T(8,128)(2,1)}, u32[]{:S(2)}) %copy-start.2) | copy-done | bytes 2097176
  88.7 0.7 shard_map.58
  89.5 3.2 %collective-permute-start.9 = (bf16[128,1024]{1,0:T(8,128)(2,1)}, bf16[128,1024]{1,0:T(8,128)(2,1)}, u32[]{:S(2)}, u32[]{:S(2)}) collective-permute-start(bf16[128,1024]{1,0:T(8,128)(2,1)} %shard_map.58), channel_id=1, source_target_pairs={{0,144},{499,2},{4,148},{503,6},{8,152},{507,10},{12,156},{511,14}... | collective-permute-start | bytes 786440 | tf_op jit(solution)/shard_map/ppermute | solution.py:273
  92.7 11.1 %all-to-all-done.1.sums_ref = bf16[8,32,1024]{2,1,0:T(8,128)(2,1)} async-done(((bf16[8,32,1024]{2,1,0:T(8,128)(2,1)}), bf16[8,32,1024]{2,1,0:T(8,128)(2,1)}, u32[]{:S(2)}, u32[]{:S(2)}) %all-to-all-start.1) | async-done | bytes 524320 | tf_op jit(solution)/shard_map/all_to_all | solution.py:70
  103.8 1.1 %shard_map.57.left_ref = bf16[48,1024]{1,0:T(8,128)(2,1)S(1)} custom-call(bf16[8,32,1024]{2,1,0:T(8,128)(2,1)} %all-to-all-done.1.sums_ref, f32[16,1024]{1,0:T(8,128)S(1)} %bitcast.23), custom_call_target="tpu_custom_call" | custom-call | tf_op jit(solution)/shard_map/pallas_call | solution.py:98
  105.0 0.8 collective-permute-done.9.refs_4_
  105.8 1.0 copy-done.4
  106.8 2.7 %shard_map.59 = (f32[16,1024]{1,0:T(8,128)}, f32[16,1024]{1,0:T(8,128)}) custom-call(bf16[48,1024]{1,0:T(8,128)(2,1)S(1)} %shard_map.57.left_ref, f32[16,1024]{1,0:T(8,128)S(1)} %bitcast.24, bf16[256,1024]{1,0:T(8,128)(2,1)S(1)} %bitcast.18, bf16[256,1024]{1,0:T(8,128)(2,1)S(1)} %bitcast.21, bf16[256,1024]{1,0:T(8,128)(2,1)S(1)} %bitcast.20, ...), custom_call_target="tpu_custom_call" | custom-call | tf_op jit(solution)/shard_map/pallas_call | solution.py:98
  (16 shorter events, 0.1 us)
Async XLA Ops:
  0.6 46.9 %copy-start = (bf16[1024,1024]{1,0:T(8,128)(2,1)S(1)}, bf16[1024,1024]{1,0:T(8,128)(2,1)}, u32[]{:S(2)}) copy-start(bf16[1024,1024]{1,0:T(8,128)(2,1)} %param.4) | copy-start | bytes 6291460
  0.6 46.9 %copy-start.1 = (bf16[1024,1024]{1,0:T(8,128)(2,1)S(1)}, bf16[1024,1024]{1,0:T(8,128)(2,1)}, u32[]{:S(2)}) copy-start(bf16[1024,1024]{1,0:T(8,128)(2,1)} %x_ref.7) | copy-start | bytes 6291460
  36.7 26.7 %collective-permute-start.2 = (bf16[2,128,1024]{2,1,0:T(8,128)(2,1)S(1)}, bf16[2,128,1024]{2,1,0:T(8,128)(2,1)S(1)}, u32[]{:S(2)}, u32[]{:S(2)}) collective-permute-start(bf16[2,128,1024]{2,1,0:T(8,128)(2,1)S(1)} %bitcast.15), channel_id=1, source_target_pairs={{0,16},{499,387},{4,20},{503,391},{8,24},{507,395},{12,28},{511,39... | collective-permute-start | bytes 1572872 | tf_op jit(solution)/shard_map/ppermute | solution.py:273
  39.0 28.7 %collective-permute-start.4 = (bf16[2,128,1024]{2,1,0:T(8,128)(2,1)S(1)}, bf16[2,128,1024]{2,1,0:T(8,128)(2,1)S(1)}, u32[]{:S(2)}, u32[]{:S(2)}) collective-permute-start(bf16[2,128,1024]{2,1,0:T(8,128)(2,1)S(1)} %bitcast.16), channel_id=1, source_target_pairs={{0,128},{499,114},{4,132},{503,118},{8,136},{507,122},{12,140},{51... | collective-permute-start | bytes 1572872 | tf_op jit(solution)/shard_map/ppermute | solution.py:273
  42.0 14.6 %collective-permute-start = (bf16[128,1024]{1,0:T(8,128)(2,1)S(1)}, bf16[128,1024]{1,0:T(8,128)(2,1)S(1)}, u32[]{:S(2)}, u32[]{:S(2)}) collective-permute-start(bf16[128,1024]{1,0:T(8,128)(2,1)S(1)} %shard_map.51.own_ref), channel_id=1, source_target_pairs={{0,144},{499,2},{4,148},{503,6},{8,152},{507,10},{12,156},{511,14}... | collective-permute-start | bytes 786440 | tf_op jit(solution)/shard_map/ppermute | solution.py:273
  51.3 22.2 %collective-permute-start.6 = (bf16[8,16,1024]{2,1,0:T(8,128)(2,1)}, bf16[8,16,1024]{2,1,0:T(8,128)(2,1)S(1)}, u32[]{:S(2)}, u32[]{:S(2)}) collective-permute-start(bf16[8,16,1024]{2,1,0:T(8,128)(2,1)} %get-tuple-element.13), channel_id=1, source_target_pairs={{0,128},{499,114},{4,132},{503,118},{8,136},{507,122},{12,140},{51... | collective-permute-start | bytes 786440 | tf_op jit(solution)/shard_map/ppermute | solution.py:273
  54.6 22.0 %collective-permute-start.7 = (bf16[8,16,1024]{2,1,0:T(8,128)(2,1)}, bf16[8,16,1024]{2,1,0:T(8,128)(2,1)S(1)}, u32[]{:S(2)}, u32[]{:S(2)}) collective-permute-start(bf16[8,16,1024]{2,1,0:T(8,128)(2,1)} %get-tuple-element.14), channel_id=1, source_target_pairs={{0,16},{499,387},{4,20},{503,391},{8,24},{507,395},{12,28},{511,39... | collective-permute-start | bytes 786440 | tf_op jit(solution)/shard_map/ppermute | solution.py:273
  56.6 20.1 %collective-permute-start.8 = (bf16[8,16,1024]{2,1,0:T(8,128)(2,1)}, bf16[8,16,1024]{2,1,0:T(8,128)(2,1)S(1)}, u32[]{:S(2)}, u32[]{:S(2)}) collective-permute-start(bf16[8,16,1024]{2,1,0:T(8,128)(2,1)} %get-tuple-element.15), channel_id=1, source_target_pairs={{0,144},{499,2},{4,148},{503,6},{8,152},{507,10},{12,156},{511,14}... | collective-permute-start | bytes 786440 | tf_op jit(solution)/shard_map/ppermute | solution.py:273
  63.4 13.3 %collective-permute-start.1 = (bf16[128,1024]{1,0:T(8,128)(2,1)S(1)}, bf16[128,1024]{1,0:T(8,128)(2,1)S(1)}, u32[]{:S(2)}, u32[]{:S(2)}) collective-permute-start(bf16[128,1024]{1,0:T(8,128)(2,1)S(1)} %get-tuple-element.11), channel_id=1, source_target_pairs={{0,144},{499,2},{4,148},{503,6},{8,152},{507,10},{12,156},{511,14}... | collective-permute-start | bytes 786440 | tf_op jit(solution)/shard_map/ppermute | solution.py:273
  67.6 14.2 %copy-start.6 = (bf16[8,16,1024]{2,1,0:T(8,128)(2,1)S(1)}, bf16[8,16,1024]{2,1,0:T(8,128)(2,1)}, u32[]{:S(2)}) copy-start(bf16[8,16,1024]{2,1,0:T(8,128)(2,1)} %get-tuple-element.12.refs_4_) | copy-start | bytes 786436
  67.6 5.8 %copy-start.3 = (bf16[2,128,1024]{2,1,0:T(8,128)(2,1)}, bf16[2,128,1024]{2,1,0:T(8,128)(2,1)S(1)}, u32[]{:S(2)}) copy-start(bf16[2,128,1024]{2,1,0:T(8,128)(2,1)S(1)} %collective-permute-done.4.rows_ref) | copy-start | bytes 1572868
  67.7 9.0 %collective-permute-start.3 = (bf16[128,1024]{1,0:T(8,128)(2,1)S(1)}, bf16[128,1024]{1,0:T(8,128)(2,1)S(1)}, u32[]{:S(2)}, u32[]{:S(2)}) collective-permute-start(bf16[128,1024]{1,0:T(8,128)(2,1)S(1)} %shard_map.53), channel_id=1, source_target_pairs={{0,16},{499,387},{4,20},{503,391},{8,24},{507,395},{12,28},{511,39... | collective-permute-start | bytes 786440 | tf_op jit(solution)/shard_map/ppermute | solution.py:273
  73.5 8.3 %collective-permute-start.5 = (bf16[128,1024]{1,0:T(8,128)(2,1)S(1)}, bf16[128,1024]{1,0:T(8,128)(2,1)S(1)}, u32[]{:S(2)}, u32[]{:S(2)}) collective-permute-start(bf16[128,1024]{1,0:T(8,128)(2,1)S(1)} %shard_map.54), channel_id=1, source_target_pairs={{0,128},{499,114},{4,132},{503,118},{8,136},{507,122},{12,140},{51... | collective-permute-start | bytes 786440 | tf_op jit(solution)/shard_map/ppermute | solution.py:273
  82.9 21.0 %copy-start.5 = (f32[1024,16]{0,1:T(8,128)S(1)}, f32[1024,16]{0,1:T(8,128)}, u32[]{:S(2)}) copy-start(f32[1024,16]{0,1:T(8,128)} %param.5) | copy-start | bytes 196612
  82.9 21.0 %all-to-all-start.1 = ((bf16[8,32,1024]{2,1,0:T(8,128)(2,1)}), bf16[8,32,1024]{2,1,0:T(8,128)(2,1)}, u32[]{:S(2)}, u32[]{:S(2)}) async-start(bf16[8,32,1024]{2,1,0:T(8,128)(2,1)} %shard_map.56), calls=%async_computation.1 | async-start | bytes 1048576 | tf_op jit(solution)/shard_map/all_to_all | solution.py:70
  87.2 1.6 %copy-start.2 = (bf16[1024,1024]{1,0:T(8,128)(2,1)S(1)}, bf16[1024,1024]{1,0:T(8,128)(2,1)}, u32[]{:S(2)}) copy-start(bf16[1024,1024]{1,0:T(8,128)(2,1)} %x_ref.7) | copy-start | bytes 6291460
  89.5 16.3 %collective-permute-start.9 = (bf16[128,1024]{1,0:T(8,128)(2,1)}, bf16[128,1024]{1,0:T(8,128)(2,1)}, u32[]{:S(2)}, u32[]{:S(2)}) collective-permute-start(bf16[128,1024]{1,0:T(8,128)(2,1)} %shard_map.58), channel_id=1, source_target_pairs={{0,144},{499,2},{4,148},{503,6},{8,152},{507,10},{12,156},{511,14}... | collective-permute-start | bytes 786440 | tf_op jit(solution)/shard_map/ppermute | solution.py:273
  105.8 1.0 copy-start.4
